TPU v7x, 32 devices: a whole 2x2x4 slice. The times are simulated.
32 devices in a mesh: row: 16 (over z, y, core), col: 2 (over x).
Axes of the slice: x: 2, y: 2, z: 4, core: 2. Of those that a mesh axis runs over, the one named last changes fastest.
Arguments:
- residues: int32 [512], P('row'), may hold values from 0 to 20
- embed_table: bfloat16 [21, 256], replicated, may hold values from -6 to 6
- conv_first: bfloat16 [4352, 256], replicated, may hold values from -0.09375 to 0.09375
- conv_second: bfloat16 [4352, 256], replicated, may hold values from -0.09375 to 0.09375
- proj_row: bfloat16 [256, 64], replicated, may hold values from -0.375 to 0.375
- proj_col: bfloat16 [256, 64], replicated, may hold values from -0.375 to 0.375
- pair_weights: bfloat16 [4, 64, 576], replicated, may hold values from -0.25 to 0.25
Outputs:
- pair_out: bfloat16 [64, 512, 512], P(None, 'row', 'col')
All inputs are finite; a program needn't handle non-finite values.
Results may differ from a plain program's by a relative error of at most 0.018.
Values may be sent and summed in bfloat16 or wider, within the bound.
A program may use at most 64 MiB of HBM per device.

v0:
```python
import functools

import jax
import jax.numpy as jnp
from jax import lax
from jax.experimental import pallas as pl
from jax.experimental.pallas import tpu as pltpu
from jax.sharding import PartitionSpec as P

MESH = pl.DeviceIdType.MESH
PAD = 8
STRIPS = 16
CHUNKS = 4
HALO = 16
F32, BF16 = jnp.float32, jnp.bfloat16


def elu(v):
    return jnp.maximum(v, jnp.exp(jnp.minimum(v, 0.0)) - 1.0)


def sequence_kernel(
    dims, res_hbm, table_hbm, w1_hbm, w2_hbm, prow_hbm, pcol_hbm, pw_hbm, left_out, right_out, bw,
    res_ref, table_ref, w1_ref, w2_ref, prow_ref, pcol_ref, pw_ref, sems, send_sem, recv_sem, tab, emb, xs, fs, cols, la, lb, right_ref,
):
    rows, ncol, span, tile, chans, kernel, layers = dims
    me_r, me_c = lax.axis_index("row"), lax.axis_index("col")
    window = rows * span
    width = table_ref.shape[1]
    half = kernel // 2
    edge = 2 * HALO
    n_row, n_col = span + 2 * edge, tile + 2 * edge
    height, wide = span + 2 * HALO, tile + 2 * HALO
    two = 2 * chans

    barrier = pltpu.get_barrier_semaphore()
    for k in range(1, rows):
        pl.semaphore_signal(
            barrier, inc=1, device_id={"row": lax.rem(me_r + k, rows)}, device_id_type=MESH
        )
    pairs = (
        (pw_hbm, pw_ref), (res_hbm, res_ref.at[me_r]), (table_hbm, table_ref), (w1_hbm, w1_ref),
        (w2_hbm, w2_ref), (prow_hbm, prow_ref), (pcol_hbm, pcol_ref),
    )
    loads = [pltpu.make_async_copy(a, b, sems.at[i]) for i, (a, b) in enumerate(pairs)]
    for load in loads:
        load.start()
    loads[0].wait()

    zero = jnp.zeros((chans, chans), BF16)
    for layer in range(layers):
        w = pw_ref[layer].astype(F32).T.astype(BF16)
        for g, offset in enumerate((0, 1, 2, -1)):
            line = []
            for tx in range(3):
                for h in range(2):
                    ty = offset - h + 1
                    tap = 3 * ty + tx
                    here = 0 <= ty <= 2
                    line.append(w[tap * chans : (tap + 1) * chans] if here else zero)
            bw[layer, g * chans : (g + 1) * chans, :] = jnp.concatenate(line, axis=1)
    n_pair = height // 2

    pl.semaphore_wait(barrier, rows - 1)
    copies = [
        pltpu.make_async_remote_copy(
            src_ref=res_hbm,
            dst_ref=res_ref.at[me_r],
            send_sem=send_sem.at[k],
            recv_sem=recv_sem.at[k],
            device_id={"row": lax.rem(me_r + k, rows)},
            device_id_type=MESH,
        )
        for k in range(1, rows)
    ]
    for copy in copies:
        copy.start()

    loads[2].wait()
    tab[...] = jnp.zeros_like(tab)
    tab[0 : table_ref.shape[0], :] = table_ref[...]
    emb[0:edge, :] = jnp.zeros((edge, width), F32)
    emb[edge + window : 2 * edge + window, :] = jnp.zeros((edge, width), F32)
    loads[1].wait()
    for copy in copies:
        copy.wait()
    per = 128 // span
    vocab = lax.broadcasted_iota(jnp.int32, (tab.shape[0], 128), 0)
    for g in range(window // 128):
        line = jnp.concatenate([res_ref[per * g + m] for m in range(per)], axis=1)
        hot = (jnp.broadcast_to(line, vocab.shape) == vocab).astype(F32).astype(BF16)
        emb[edge + 128 * g : edge + 128 * (g + 1), :] = lax.dot_general(
            hot, tab[...], (((0,), (0,)), ((), ())), preferred_element_type=F32
        )
    xs[0:n_row, :] = emb[pl.ds(pl.multiple_of(me_r * span, span), n_row), :]
    xs[n_row : n_row + n_col, :] = emb[pl.ds(pl.multiple_of(me_c * tile, tile), n_col), :]

    n_first = n_row + n_col - 2 * half
    n_second = n_first - 2 * half
    for k in range(kernel):
        cols[:, k * width : (k + 1) * width] = xs[k : k + n_first, :].astype(BF16)
    loads[3].wait()
    first = elu(jnp.dot(cols[...], w1_ref[...], preferred_element_type=F32))
    at = lax.broadcasted_iota(jnp.int32, (n_first, width), 0) + half
    pos = at + jnp.where(at < n_row, me_r * span - edge, me_c * tile - edge - n_row)
    first = jnp.where((pos >= 0) & (pos < window), first, 0.0)
    fs[...] = first.astype(BF16).astype(F32)
    for k in range(kernel):
        cols[0:n_second, k * width : (k + 1) * width] = fs[k : k + n_second, :].astype(BF16)
    loads[4].wait()
    second = elu(jnp.dot(cols[0:n_second, :], w2_ref[...], preferred_element_type=F32))
    second = (fs[half : half + n_second, :] + second).astype(BF16)

    loads[5].wait()
    loads[6].wait()
    blank = jnp.zeros((chans, width), BF16)
    pr, pc = prow_ref[...], pcol_ref[...]
    s_row, s_col = second[0:height], second[n_row : n_row + wide]
    dot = functools.partial(jnp.dot, preferred_element_type=F32)

    def project(x, *parts):
        w = jnp.concatenate(parts, axis=0)
        y = lax.dot_general(x, w, (((1,), (1,)), ((), ())), preferred_element_type=F32)
        return y.astype(BF16).astype(F32)

    la[...] = project(s_row, pr, blank)
    lb[...] = project(s_row, blank, pr)
    right_ref[...] = project(s_col, pc, pc)
    left_out[...] = la[pl.ds(0, n_pair, stride=2), :] + lb[pl.ds(1, n_pair, stride=2), :]
    slabs = wide // STRIPS
    for m in range(slabs):
        right_out[STRIPS * m : STRIPS * (m + 1)] = right_ref[pl.ds(m, STRIPS, stride=slabs), :]


def pair_kernel(
    dims, left_ref, right_ref, bw_hbm, out_hbm, bw, pair, act_a, act_b, lin, stage, outv, masks, sems
):
    rows, ncol, span, tile, chans, layers = dims
    me_r, me_c = lax.axis_index("row"), lax.axis_index("col")
    n_pair = (span + 2 * HALO) // 2
    wide, two = tile + 2 * HALO, 2 * chans
    slabs = wide // STRIPS
    load = pltpu.make_async_copy(bw_hbm, bw, sems.at[0])
    load.start()

    at = lax.broadcasted_iota(jnp.int32, (wide, two), 0)
    col = lax.rem(at, STRIPS) * slabs + lax.div(at, STRIPS)
    inside = ((col >= HALO) | (me_c > 0)) & ((col < HALO + tile) | (me_c < ncol - 1))
    inside = jnp.where(inside, 1.0, 0.0)
    masks[0] = inside.astype(BF16)
    masks[1] = (inside * (me_r > 0).astype(F32)).astype(BF16)
    masks[2] = (inside * (me_r < rows - 1).astype(F32)).astype(BF16)
    blank = jnp.zeros((PAD, wide, two), BF16)
    for act in (act_a, act_b):
        act[0:PAD] = blank
        act[PAD + n_pair : 2 * PAD + n_pair] = blank
    lane = lax.broadcasted_iota(jnp.int32, (wide, two), 1)
    low_bf16 = lane.astype(F32).astype(BF16) < jnp.asarray(chans, BF16)
    low_half = lane < chans

    def put(act, p, value):
        pair[p] = value
        which = 1 if p < HALO // 2 else 2 if p >= n_pair - HALO // 2 else 0
        act[p + PAD] = elu(value).astype(BF16) * masks[which]

    def start(p):
        put(act_a, p, right_ref[...] + left_ref[p : p + 1, :])

    def add(p, m, part):
        at = pl.ds(STRIPS * m, STRIPS)
        pair[p, at, :] = pair[p, at, :] + part

    def conv(layer, src, d, slots):
        lhs = jnp.concatenate(
            [
                jnp.concatenate(
                    [src[p + PAD], jnp.where(low_bf16, src[p + PAD + d], src[p + PAD - d])], axis=1
                )
                for p in slots
            ],
            axis=0,
        )
        got = jnp.dot(lhs, bw[layer], preferred_element_type=F32)
        for k, p in enumerate(slots):
            for m in range(slabs):
                row = got[k * wide + STRIPS * m : k * wide + STRIPS * (m + 1)]
                to = m + d
                part = row[:, 0:two]
                add(p, to % slabs, part if to < slabs else pltpu.roll(part, 1, 0))
                add(p, m, row[:, two : 2 * two])
                to = m - d
                part = row[:, 2 * two : 3 * two]
                add(p, to % slabs, part if to >= 0 else pltpu.roll(part, STRIPS - 1, 0))
        return [pair[p] for p in slots]

    bufs = (act_a, act_b)
    for layer in range(layers - 1):
        src, dst = bufs[layer % 2], bufs[(layer + 1) % 2]
        d = 2**layer
        units = [(q + d, n_pair - 2 * d + q) for q in range(d)]
        n_rim = len(units)
        units += [
            (2 * d * (q // d) + q % d, 2 * d * (q // d) + q % d + d)
            for q in range(d, n_pair // 2 - d)
        ]
        if layer == 0:
            for p in range(n_pair):
                start(p)
            load.wait()
        for u, slots in enumerate(units):
            one, other = conv(layer, src, d, slots)
            if u < n_rim:
                new = [pltpu.roll(one, chans, 1), one, other, pltpu.roll(other, chans, 1)]
                slots = [u, u + d, n_pair - 2 * d + u, n_pair - d + u]
            else:
                new = [
                    jnp.where(low_half, one, pltpu.roll(other, chans, 1)),
                    jnp.where(low_half, pltpu.roll(one, chans, 1), other),
                ]
            for p, value in zip(slots, new):
                put(dst, p, value)

    src = bufs[(layers - 1) % 2]
    d = 2 ** (layers - 1)
    halves = tile // 128
    for u in range((n_pair - HALO) // 2):
        slots = (HALO // 2 + 2 * u, HALO // 2 + 2 * u + 1)
        for k, value in enumerate(conv(layers - 1, src, d, slots)):
            b = lin.at[(2 * u + k) % 4]
            for m in range(slabs):
                b[pl.ds(m, STRIPS, stride=slabs), :] = value[STRIPS * m : STRIPS * (m + 1)]
            turned = b[HALO : HALO + tile, :].T
            at = slots[k] - HALO // 2
            line = 2 * d * (at // d) + at % d
            for h in range(halves):
                block = turned[:, 128 * h : 128 * (h + 1)]
                stage[h, pl.ds(line, chans, stride=span), :] = block[0:chans]
                stage[h, pl.ds(line + d, chans, stride=span), :] = block[chans:two]
    step = chans // CHUNKS
    saves = []
    for g in range(CHUNKS):
        for c in range(g * step, (g + 1) * step):
            for h in range(halves):
                outv[c, :, 128 * h : 128 * (h + 1)] = stage[h, c * span : (c + 1) * span, :].astype(BF16)
        part = pl.ds(g * step, step)
        saves.append(pltpu.make_async_copy(outv.at[part], out_hbm.at[part], sems.at[1 + g]))
        saves[-1].start()
    for save in saves:
        save.wait()


def local(residues, embed_table, conv_first, conv_second, proj_row, proj_col, pair_weights):
    rows, ncol = lax.axis_size("row"), lax.axis_size("col")
    span = residues.shape[0]
    window = span * rows
    tile = window // ncol
    width = embed_table.shape[1]
    chans = proj_row.shape[1]
    layers = pair_weights.shape[0]
    kernel = conv_first.shape[0] // width
    half = kernel // 2
    edge = 2 * HALO
    total = span + tile + 4 * edge
    height, wide = span + 2 * HALO, tile + 2 * HALO
    n_pair = height // 2
    two = 2 * chans
    vmem = pl.BlockSpec(memory_space=pltpu.VMEM)
    hbm = pl.BlockSpec(memory_space=pltpu.HBM)
    left, right, weights = pl.pallas_call(
        functools.partial(sequence_kernel, (rows, ncol, span, tile, chans, kernel, layers)),
        out_shape=(
            jax.ShapeDtypeStruct((n_pair, two), F32),
            jax.ShapeDtypeStruct((wide, two), F32),
            jax.ShapeDtypeStruct((layers, 4 * chans, 6 * chans), BF16),
        ),
        in_specs=[hbm] * 7,
        out_specs=(vmem, vmem, vmem),
        scratch_shapes=[
            pltpu.VMEM((rows, 1, span), jnp.int32),
            pltpu.VMEM(embed_table.shape, BF16),
            pltpu.VMEM(conv_first.shape, BF16),
            pltpu.VMEM(conv_second.shape, BF16),
            pltpu.VMEM((chans, width), BF16),
            pltpu.VMEM((chans, width), BF16),
            pltpu.VMEM(pair_weights.shape, BF16),
            pltpu.SemaphoreType.DMA((7,)),
            pltpu.SemaphoreType.DMA((rows,)),
            pltpu.SemaphoreType.DMA((rows,)),
            pltpu.VMEM((32, width), BF16),
            pltpu.VMEM((window + 2 * edge, width), F32),
            pltpu.VMEM((total, width), F32),
            pltpu.VMEM((total - 2 * half, width), F32),
            pltpu.VMEM((total - 2 * half, kernel * width), BF16),
            pltpu.VMEM((height, two), F32),
            pltpu.VMEM((height, two), F32),
            pltpu.VMEM((wide, two), F32),
        ],
        compiler_params=pltpu.CompilerParams(
            vmem_limit_bytes=60 * 1024 * 1024, collective_id=0, has_side_effects=True
        ),
        name="sequence",
    )(residues.reshape(1, span), embed_table, conv_first, conv_second, proj_row.T, proj_col.T, pair_weights)
    return pl.pallas_call(
        functools.partial(pair_kernel, (rows, ncol, span, tile, chans, layers)),
        out_shape=jax.ShapeDtypeStruct((chans, span, tile), BF16),
        in_specs=[vmem, vmem, hbm],
        out_specs=hbm,
        scratch_shapes=[
            pltpu.VMEM((layers, 4 * chans, 6 * chans), BF16),
            pltpu.VMEM((n_pair, wide, two), F32),
            pltpu.VMEM((n_pair + 2 * PAD, wide, two), BF16),
            pltpu.VMEM((n_pair + 2 * PAD, wide, two), BF16),
            pltpu.VMEM((4, wide, two), F32),
            pltpu.VMEM((tile // 128, chans * span, 128), F32),
            pltpu.VMEM((chans, span, tile), BF16),
            pltpu.VMEM((3, wide, two), BF16),
            pltpu.SemaphoreType.DMA((1 + CHUNKS,)),
        ],
        compiler_params=pltpu.CompilerParams(vmem_limit_bytes=40000 * 1024),
        name="pairs",
    )(left, right, weights)


def solution(mesh):
    return jax.shard_map(
        local,
        mesh=mesh,
        in_specs=(P("row"), P(), P(), P(), P(), P(), P()),
        out_specs=P(None, "row", "col"),
        check_vma=False,
    )
```

profile of v0, /device:TPU:0, one launch (start us, length us, event | category | flops | bytes accessed | tf_op | source)
XLA Modules:
  0.0 32.7 jit_solution(10700540167674213291)
XLA Ops:
  0.0 15.7 %sequence.1 = (f32[32,128]{1,0:T(8,128)}, f32[288,128]{1,0:T(8,128)}, bf16[4,256,384]{2,1,0:T(8,128)(2,1)}) custom-call(s32[1,32]{1,0:T(1,128)} %bitcast.5, bf16[21,256]{1,0:T(8,128)(2,1)} %table_hbm.1, bf16[4352,256]{1,0:T(8,128)(2,1)} %w1_hbm.1, bf16[4352,256]{1,0:T(8,128)(2,1)} %w2_hbm.1, bf16[64,256]{1,0:T(8,128)(2,1)} %bitcast.3, ...), custom_call_target="tpu_custom_call" | custom-call | tf_op jit(solution)/shard_map/sequence/pallas_call | solution.py:269
  15.7 0.0 copy-start
  15.7 1.1 %copy-done = bf16[4,256,384]{2,1,0:T(8,128)(2,1)S(1)} copy-done((bf16[4,256,384]{2,1,0:T(8,128)(2,1)S(1)}, bf16[4,256,384]{2,1,0:T(8,128)(2,1)}, u32[]{:S(2)}) %copy-start) | copy-done | bytes 786456
  16.8 0.0 copy-start.1
  16.8 0.9 %copy-done.1 = f32[288,128]{1,0:T(8,128)S(1)} copy-done((f32[288,128]{1,0:T(8,128)S(1)}, f32[288,128]{1,0:T(8,128)}, u32[]{:S(2)}) %copy-start.1) | copy-done | bytes 147480
  17.7 0.0 copy-start.2
  17.7 0.7 %copy-done.2 = f32[32,128]{1,0:T(8,128)S(1)} copy-done((f32[32,128]{1,0:T(8,128)S(1)}, f32[32,128]{1,0:T(8,128)}, u32[]{:S(2)}) %copy-start.2) | copy-done | bytes 16408
  18.5 14.1 %pairs.1 = bf16[64,32,256]{2,1,0:T(8,128)(2,1)} custom-call(f32[32,128]{1,0:T(8,128)S(1)} %copy-done.2, f32[288,128]{1,0:T(8,128)S(1)} %copy-done.1, bf16[4,256,384]{2,1,0:T(8,128)(2,1)S(1)} %copy-done), custom_call_target="tpu_custom_call" | custom-call | tf_op jit(solution)/shard_map/pairs/pallas_call | solution.py:303
Async XLA Ops:
  15.7 1.1 %copy-start = (bf16[4,256,384]{2,1,0:T(8,128)(2,1)S(1)}, bf16[4,256,384]{2,1,0:T(8,128)(2,1)}, u32[]{:S(2)}) copy-start(bf16[4,256,384]{2,1,0:T(8,128)(2,1)} %get-tuple-element.10.bw_hbm) | copy-start | bytes 2359300
  16.8 0.9 %copy-start.1 = (f32[288,128]{1,0:T(8,128)S(1)}, f32[288,128]{1,0:T(8,128)}, u32[]{:S(2)}) copy-start(f32[288,128]{1,0:T(8,128)} %get-tuple-element.9.right_ref) | copy-start | bytes 442372
  17.7 0.7 %copy-start.2 = (f32[32,128]{1,0:T(8,128)S(1)}, f32[32,128]{1,0:T(8,128)}, u32[]{:S(2)}) copy-start(f32[32,128]{1,0:T(8,128)} %get-tuple-element.8.left_ref) | copy-start | bytes 49156
where the time goes:
time: 33 us; the launch traced here: 32.7 us
  Pallas kernels  29.8 us (90%)
  local copies, waits for them, and re-layouts  2.75 us (8%)
    pallas_call x1, Pallas kernels, local(): pl.pallas_call(functools.partial(sequence_kernel, (rows, ncol, span, tile...  15.7 us
    pallas_call x1, Pallas kernels, local(): pl.pallas_call(functools.partial(pair_kernel, (rows, ncol, span, tile, ch...  14.1 us
    unnamed x6, local copies, waits for them, and re-layouts  2.75 us

commit v1 on v0

v1 whole, which is shorter than its diff:
```python
import functools

import jax
import jax.numpy as jnp
from jax import lax
from jax.experimental import pallas as pl
from jax.experimental.pallas import tpu as pltpu
from jax.sharding import PartitionSpec as P

MESH = pl.DeviceIdType.MESH
STRIPS = 16
CHUNKS = 4
STEP = 18
LIMIT = 67043328
TAPS = 4
HALO = 16
F32, BF16 = jnp.float32, jnp.bfloat16


def elu(v):
    return jnp.maximum(v, jnp.exp(jnp.minimum(v, 0.0)) - 1.0)


def sequence_kernel(
    dims, res_hbm, table_hbm, w1_hbm, w2_hbm, prow_hbm, pcol_hbm, pw_hbm, left_out, right_out, bw,
    res_ref, table_ref, w1_ref, w2_ref, prow_ref, pcol_ref, pw_ref, sems, send_sem, recv_sem,
    taps, fs, tmp, right_ref,
):
    rows, ncol, span, tile, chans, kernel, layers = dims
    me_r, me_c = lax.axis_index("row"), lax.axis_index("col")
    window = rows * span
    vocab, width = table_ref.shape
    half = kernel // 2
    edge = 2 * HALO
    n_row, n_col = span + 2 * edge, tile + 2 * edge
    height, wide = span + 2 * HALO, tile + 2 * HALO
    two = 2 * chans

    around, per_col = edge // span, tile // span
    low, high = me_c * per_col - around, (me_c + 1) * per_col + around

    def takes(source, target):
        near = (source - target <= around) & (target - source <= around)
        return near | ((source >= low) & (source < high))

    peers = [lax.rem(me_r + k, rows) for k in range(1, rows)]
    barrier = pltpu.get_barrier_semaphore()
    for peer in peers:

        @pl.when(takes(peer, me_r))
        def _(peer=peer):
            pl.semaphore_signal(barrier, inc=1, device_id={"row": peer}, device_id_type=MESH)

    pairs = (
        (res_hbm, res_ref.at[me_r]), (table_hbm, table_ref), (w1_hbm, w1_ref), (pw_hbm, pw_ref),
        (w2_hbm, w2_ref), (prow_hbm, prow_ref), (pcol_hbm, pcol_ref),
    )
    loads = [pltpu.make_async_copy(a, b, sems.at[i]) for i, (a, b) in enumerate(pairs)]
    for load in loads:
        load.start()

    expected = sum(takes(me_r, peer).astype(jnp.int32) for peer in peers)
    pl.semaphore_wait(barrier, expected)
    copies = [
        pltpu.make_async_remote_copy(
            src_ref=res_hbm,
            dst_ref=res_ref.at[me_r],
            send_sem=send_sem.at[k],
            recv_sem=recv_sem.at[k],
            device_id={"row": peer},
            device_id_type=MESH,
        )
        for k, peer in enumerate(peers)
    ]
    for copy, peer in zip(copies, peers):

        @pl.when(takes(me_r, peer))
        def _(copy=copy):
            copy.start()

    slot = 1 << (vocab - 1).bit_length()
    share = 128 // slot
    groups = -(-kernel // share)
    loads[1].wait()
    loads[2].wait()
    table = jnp.concatenate([table_ref[...], jnp.zeros((slot - vocab, width), BF16)], axis=0)
    for k in range(kernel):
        row = jnp.dot(table, w1_ref[k * width : (k + 1) * width, :], preferred_element_type=F32)
        taps[k * slot : (k + 1) * slot, :] = row.astype(BF16)
    taps[kernel * slot :, :] = jnp.zeros((groups * 128 - kernel * slot, width), BF16)

    loads[3].wait()
    zero = jnp.zeros((chans, chans), BF16)
    for layer in range(layers):
        w = pw_ref[layer].astype(F32).T.astype(BF16)
        for g, offset in enumerate((0, 1, 2, -1)):
            line = []
            for tx in range(3):
                for h in range(2):
                    ty = offset - h + 1
                    tap = 3 * ty + tx
                    here = 0 <= ty <= 2
                    line.append(w[tap * chans : (tap + 1) * chans] if here else zero)
            bw[layer, g * chans : (g + 1) * chans, :] = jnp.concatenate(line, axis=1)
    for load in loads[4:]:
        load.wait()

    loads[0].wait()
    for k, copy in enumerate(copies):
        source = lax.rem(me_r + rows - 1 - k, rows)

        @pl.when(takes(source, me_r))
        def _(copy=copy):
            copy.wait_recv()

        @pl.when(takes(me_r, peers[k]))
        def _(copy=copy):
            copy.wait_send()

    shards = [me_r + i - around for i in range(n_row // span)]
    shards += [low + i for i in range(n_col // span)]
    pieces = []
    for shard in shards:
        piece = res_ref[jnp.clip(shard, 0, rows - 1)]
        pieces.append(jnp.where((shard >= 0) & (shard < rows), piece, -1).astype(F32))
    total = n_row + n_col
    padded = -(-(total + 8) // 128) * 128
    if padded > total:
        pieces.append(jnp.full((1, padded - total), -1.0, F32))
    line = jnp.concatenate(pieces, axis=1)
    one = jnp.ones((128, 128), BF16)
    at = lax.broadcasted_iota(jnp.int32, (128, 128), 0)
    lane = lax.broadcasted_iota(jnp.int32, (128, 128), 1)
    for g in range(padded // 128):
        diagonal = jnp.where(at == lane, line[:, 128 * g : 128 * (g + 1)], 0.0).astype(BF16)
        tmp[128 * g : 128 * (g + 1), :] = jnp.dot(diagonal, one, preferred_element_type=F32)
    n_first = total - 2 * half
    reach = n_first + share * (groups - 1)
    lanes = lax.broadcasted_iota(jnp.int32, (reach, 128), 1)
    seen = tmp[0:reach, :]
    for i in range(1, share):
        seen = jnp.where(lanes < slot * i, seen, tmp[i : i + reach, :])
    fs[0:reach, 0:128] = seen
    kind = lax.rem(lax.broadcasted_iota(jnp.int32, (n_first, 128), 1), slot).astype(F32)
    hot = jnp.concatenate(
        [
            jnp.where(fs[share * g : share * g + n_first, 0:128] == kind, 1.0, 0.0).astype(BF16)
            for g in range(groups)
        ],
        axis=1,
    )
    first = elu(jnp.dot(hot, taps[...], preferred_element_type=F32))
    at = lax.broadcasted_iota(jnp.int32, (n_first, width), 0) + half
    pos = at + jnp.where(at < n_row, me_r * span - edge, me_c * tile - edge - n_row)
    first = jnp.where((pos >= 0) & (pos < window), first, 0.0)
    fs[0:n_first, :] = first.astype(BF16).astype(F32)

    acc = None
    for g in range(0, kernel, TAPS):
        some = range(g, min(g + TAPS, kernel))
        lhs = jnp.concatenate(
            [
                jnp.concatenate(
                    [fs[k : k + height, :], fs[k + n_row : k + n_row + wide, :]], axis=0
                ).astype(BF16)
                for k in some
            ],
            axis=1,
        )
        w2 = w2_ref[g * width : (some[-1] + 1) * width, :]
        got = jnp.dot(lhs, w2, preferred_element_type=F32)
        acc = got if acc is None else acc + got
    centre = jnp.concatenate(
        [fs[half : half + height, :], fs[half + n_row : half + n_row + wide, :]], axis=0
    )
    second = (centre + elu(acc)).astype(BF16)

    def project(x, w):
        both = jnp.concatenate([w, w], axis=0)
        y = lax.dot_general(x, both, (((1,), (1,)), ((), ())), preferred_element_type=F32)
        return y.astype(BF16).astype(F32)

    tmp[0:height, :] = project(second[0:height], prow_ref[...])
    right_ref[...] = project(second[height : height + wide], pcol_ref[...])
    n_pair = height // 2
    half_lane = lax.broadcasted_iota(jnp.int32, (n_pair, two), 1) < chans
    left_out[...] = jnp.where(
        half_lane, tmp[pl.ds(0, n_pair, stride=2), :], tmp[pl.ds(1, n_pair, stride=2), :]
    )
    slabs = wide // STRIPS
    for m in range(slabs):
        right_out[STRIPS * m : STRIPS * (m + 1)] = right_ref[pl.ds(m, STRIPS, stride=slabs), :]


def pair_kernel(
    dims, left_hbm, right_hbm, bw_hbm, out_hbm, left_ref, right_ref, bw, pair, act_a, act_b, lin, stage, outv, masks, sems
):
    rows, ncol, span, tile, chans, layers = dims
    me_r, me_c = lax.axis_index("row"), lax.axis_index("col")
    n_pair = (span + 2 * HALO) // 2
    wide, two = tile + 2 * HALO, 2 * chans
    slabs = wide // STRIPS
    moves = ((left_hbm, left_ref), (right_hbm, right_ref), (bw_hbm, bw))
    loads = [pltpu.make_async_copy(a, b, sems.at[i]) for i, (a, b) in enumerate(moves)]
    for load in loads:
        load.start()

    at = lax.broadcasted_iota(jnp.int32, (wide, two), 0)
    col = lax.rem(at, STRIPS) * slabs + lax.div(at, STRIPS)
    inside = ((col >= HALO) | (me_c > 0)) & ((col < HALO + tile) | (me_c < ncol - 1))
    inside = jnp.where(inside, 1.0, 0.0)
    masks[0] = inside.astype(BF16)
    masks[1] = (inside * (me_r > 0).astype(F32)).astype(BF16)
    masks[2] = (inside * (me_r < rows - 1).astype(F32)).astype(BF16)
    lane = lax.broadcasted_iota(jnp.int32, (wide, two), 1)
    low_bf16 = lane.astype(F32).astype(BF16) < jnp.asarray(chans, BF16)
    low_half = lane < chans

    def put(act, p, value):
        pair[p] = value
        if isinstance(p, int):
            which = 1 if p < HALO // 2 else 2 if p >= n_pair - HALO // 2 else 0
        else:
            which = jnp.where(p < HALO // 2, 1, jnp.where(p >= n_pair - HALO // 2, 2, 0))
        act[p] = elu(value).astype(BF16) * masks[which]

    def start(p):
        put(act_a, p, right_ref[...] + left_ref[pl.ds(p, 1), :])

    def shifted(part, d):
        if d > 0:
            ends = [part[STRIPS * m : STRIPS * (m + 1)] for m in range(slabs - d, slabs)]
            ends = [pltpu.roll(e, 1, 0) for e in ends]
            return jnp.concatenate(ends + [part[: STRIPS * (slabs - d)]], axis=0)
        ends = [part[STRIPS * m : STRIPS * (m + 1)] for m in range(-d)]
        ends = [pltpu.roll(e, STRIPS - 1, 0) for e in ends]
        return jnp.concatenate([part[STRIPS * -d :]] + ends, axis=0)

    def conv(layer, src, d, slots):
        lhs = jnp.concatenate(
            [
                jnp.concatenate(
                    [src[p], jnp.where(low_bf16, src[p + d], src[p - d])], axis=1
                )
                for p in slots
            ],
            axis=0,
        )
        got = jnp.dot(lhs, bw[layer], preferred_element_type=F32)
        values = []
        for k, p in enumerate(slots):
            part = got[k * wide : (k + 1) * wide]
            total = shifted(part[:, 0:two], d) + part[:, two : 2 * two]
            total = total + shifted(part[:, 2 * two : 3 * two], -d)
            values.append(pair[p] + total)
        return values

    loads[0].wait()
    loads[1].wait()
    bufs = (act_a, act_b)
    for layer in range(layers - 1):
        src, dst = bufs[layer % 2], bufs[(layer + 1) % 2]
        d = 2**layer
        if layer == 0:
            def begin(p, _):
                start(p)
                return 0

            lax.fori_loop(0, n_pair, begin, 0, unroll=4)
            loads[2].wait()

        def step(q, _, rim=False, layer=layer, src=src, dst=dst, d=d):
            if rim:
                slots = [q + d, n_pair - 2 * d + q]
            else:
                x = 2 * d * lax.div(q, d) + lax.rem(q, d)
                slots = [x, x + d]
            one, other = conv(layer, src, d, slots)
            if rim:
                new = [pltpu.roll(one, chans, 1), one, other, pltpu.roll(other, chans, 1)]
                slots = [q, q + d, n_pair - 2 * d + q, n_pair - d + q]
            else:
                new = [
                    jnp.where(low_half, one, pltpu.roll(other, chans, 1)),
                    jnp.where(low_half, pltpu.roll(one, chans, 1), other),
                ]
            for p, value in zip(slots, new):
                put(dst, p, value)
            return 0

        n_main = n_pair // 2 - 2 * d
        lax.fori_loop(d, d + n_main, step, 0, unroll=n_main // 2)
        for q in range(d):
            step(q, 0, rim=True)

    src = bufs[(layers - 1) % 2]
    d = 2 ** (layers - 1)
    halves = tile // 128
    for u in range((n_pair - HALO) // 2):
        slots = (HALO // 2 + 2 * u, HALO // 2 + 2 * u + 1)
        for k, value in enumerate(conv(layers - 1, src, d, slots)):
            b = lin.at[(2 * u + k) % 4]
            for m in range(slabs):
                b[pl.ds(m, STRIPS, stride=slabs), :] = value[STRIPS * m : STRIPS * (m + 1)]
            turned = b[HALO : HALO + tile, :].T
            at = slots[k] - HALO // 2
            line = 2 * d * (at // d) + at % d
            for h in range(halves):
                block = turned[:, 128 * h : 128 * (h + 1)]
                for i, rows_of in ((line, block[0:chans]), (line + d, block[chans:two])):
                    stage[h, i // 16, pl.ds(i % 16, chans, stride=STEP), :] = rows_of
    step = chans // CHUNKS
    saves = []
    for g in range(CHUNKS):
        for c in range(g * step, (g + 1) * step):
            for h in range(halves):
                for r in range(span // 16):
                    got = stage[h, r, STEP * c : STEP * c + 16, :]
                    outv[c, 16 * r : 16 * (r + 1), 128 * h : 128 * (h + 1)] = got.astype(BF16)
        part = pl.ds(g * step, step)
        saves.append(pltpu.make_async_copy(outv.at[part], out_hbm.at[part], sems.at[3 + g]))
        saves[-1].start()
    for save in saves:
        save.wait()


def local(residues, embed_table, conv_first, conv_second, proj_row, proj_col, pair_weights):
    rows, ncol = lax.axis_size("row"), lax.axis_size("col")
    span = residues.shape[0]
    window = span * rows
    tile = window // ncol
    width = embed_table.shape[1]
    chans = proj_row.shape[1]
    layers = pair_weights.shape[0]
    kernel = conv_first.shape[0] // width
    edge = 2 * HALO
    slot = 1 << (embed_table.shape[0] - 1).bit_length()
    padded = -(-(span + tile + 4 * edge + 8) // 128) * 128
    height, wide = span + 2 * HALO, tile + 2 * HALO
    n_pair = height // 2
    two = 2 * chans
    vmem = pl.BlockSpec(memory_space=pltpu.VMEM)
    hbm = pl.BlockSpec(memory_space=pltpu.HBM)
    left, right, weights = pl.pallas_call(
        functools.partial(sequence_kernel, (rows, ncol, span, tile, chans, kernel, layers)),
        out_shape=(
            jax.ShapeDtypeStruct((n_pair, two), F32),
            jax.ShapeDtypeStruct((wide, two), F32),
            jax.ShapeDtypeStruct((layers, 4 * chans, 6 * chans), BF16),
        ),
        in_specs=[hbm] * 7,
        out_specs=(vmem, vmem, vmem),
        scratch_shapes=[
            pltpu.VMEM((rows, 1, span), jnp.int32),
            pltpu.VMEM(embed_table.shape, BF16),
            pltpu.VMEM(conv_first.shape, BF16),
            pltpu.VMEM(conv_second.shape, BF16),
            pltpu.VMEM((chans, width), BF16),
            pltpu.VMEM((chans, width), BF16),
            pltpu.VMEM(pair_weights.shape, BF16),
            pltpu.SemaphoreType.DMA((7,)),
            pltpu.SemaphoreType.DMA((rows,)),
            pltpu.SemaphoreType.DMA((rows,)),
            pltpu.VMEM((-(-kernel * slot // 128) * 128, width), BF16),
            pltpu.VMEM((padded, width), F32),
            pltpu.VMEM((padded, two), F32),
            pltpu.VMEM((wide, two), F32),
        ],
        compiler_params=pltpu.CompilerParams(
            vmem_limit_bytes=LIMIT, collective_id=0, has_side_effects=True
        ),
        name="sequence",
    )(residues.reshape(1, span), embed_table, conv_first, conv_second, proj_row.T, proj_col.T, pair_weights)
    return pl.pallas_call(
        functools.partial(pair_kernel, (rows, ncol, span, tile, chans, layers)),
        out_shape=jax.ShapeDtypeStruct((chans, span, tile), BF16),
        in_specs=[hbm] * 3,
        out_specs=hbm,
        scratch_shapes=[
            pltpu.VMEM((n_pair, two), F32),
            pltpu.VMEM((wide, two), F32),
            pltpu.VMEM((layers, 4 * chans, 6 * chans), BF16),
            pltpu.VMEM((n_pair, wide, two), F32),
            pltpu.VMEM((n_pair, wide, two), BF16),
            pltpu.VMEM((n_pair, wide, two), BF16),
            pltpu.VMEM((4, wide, two), F32),
            pltpu.VMEM((tile // 128, span // 16, chans * STEP, 128), F32),
            pltpu.VMEM((chans, span, tile), BF16),
            pltpu.VMEM((3, wide, two), BF16),
            pltpu.SemaphoreType.DMA((3 + CHUNKS,)),
        ],
        compiler_params=pltpu.CompilerParams(vmem_limit_bytes=LIMIT),
        name="pairs",
    )(left, right, weights)


def solution(mesh):
    return jax.shard_map(
        local,
        mesh=mesh,
        in_specs=(P("row"), P(), P(), P(), P(), P(), P()),
        out_specs=P(None, "row", "col"),
        check_vma=False,
    )
```

time: 33 us -> 26 us (0.79)
  Pallas kernels: 29.8 us -> 25.8 us
  local copies, waits for them, and re-layouts: 2.75 us -> 0 us
    pallas_call x1, Pallas kernels: 15.7 us -> 12 us  [local(): pl.pallas_call(functools.partial(sequence_kernel, (rows, ncol, span, tile...]
    unnamed x6 -> x0, local copies, waits for them, and re-layouts: 2.75 us -> none
    pallas_call x1, Pallas kernels: 14.1 us -> 13.8 us  [local(): pl.pallas_call(functools.partial(pair_kernel, (rows, ncol, span, tile, ch...]
where the time goes in v1:
time: 26 us; the launch traced here: 25.8 us
  Pallas kernels  25.8 us (99%)
    pallas_call x1, Pallas kernels, local(): pl.pallas_call(functools.partial(pair_kernel, (rows, ncol, span, tile, ch...  13.8 us
    pallas_call x1, Pallas kernels, local(): pl.pallas_call(functools.partial(sequence_kernel, (rows, ncol, span, tile...  12 us

profile of v1, /device:TPU:0, one launch (start us, length us, event | category | flops | bytes accessed | tf_op | source)
XLA Modules:
  0.0 25.8 jit_solution(6264963180332191635)
XLA Ops:
  0.0 12.0 %sequence.1 = (f32[32,128]{1,0:T(8,128)}, f32[288,128]{1,0:T(8,128)}, bf16[4,256,384]{2,1,0:T(8,128)(2,1)}) custom-call(s32[1,32]{1,0:T(1,128)} %bitcast.5, bf16[21,256]{1,0:T(8,128)(2,1)} %table_hbm.1, bf16[4352,256]{1,0:T(8,128)(2,1)} %w1_hbm.1, bf16[4352,256]{1,0:T(8,128)(2,1)} %w2_hbm.1, bf16[64,256]{1,0:T(8,128)(2,1)} %bitcast.3, ...), custom_call_target="tpu_custom_call" | custom-call | tf_op jit(solution)/shard_map/sequence/pallas_call | solution.py:344
  12.0 13.8 %pairs.1 = bf16[64,32,256]{2,1,0:T(8,128)(2,1)} custom-call(f32[32,128]{1,0:T(8,128)} %get-tuple-element.8.left_hbm, f32[288,128]{1,0:T(8,128)} %get-tuple-element.9.right_hbm, bf16[4,256,384]{2,1,0:T(8,128)(2,1)} %get-tuple-element.10.bw_hbm), custom_call_target="tpu_custom_call" | custom-call | tf_op jit(solution)/shard_map/pairs/pallas_call | solution.py:374

commit v2 on v1

--- a/solution.py
+++ b/solution.py
@@ -9,9 +9,8 @@
 
 MESH = pl.DeviceIdType.MESH
 STRIPS = 16
-CHUNKS = 4
 STEP = 18
-LIMIT = 67043328
+LIMIT = 67043328 - 163840
 TAPS = 4
 HALO = 16
 F32, BF16 = jnp.float32, jnp.bfloat16
@@ -22,9 +21,9 @@
 
 
 def sequence_kernel(
-    dims, res_hbm, table_hbm, w1_hbm, w2_hbm, prow_hbm, pcol_hbm, pw_hbm, left_out, right_out, bw,
-    res_ref, table_ref, w1_ref, w2_ref, prow_ref, pcol_ref, pw_ref, sems, send_sem, recv_sem,
-    taps, fs, tmp, right_ref,
+    dims, res_hbm, table_hbm, w1_hbm, w2_hbm, prow_hbm, pcol_hbm, pw_hbm, left_out, right_out, bw_out,
+    res_ref, table_ref, w1_ref, w2_ref, prow_ref, pcol_ref, pw_ref, sems, send_sem, recv_sem, ready,
+    taps, fs, tmp, right_ref, bw,
 ):
     rows, ncol, span, tile, chans, kernel, layers = dims
     me_r, me_c = lax.axis_index("row"), lax.axis_index("col")
@@ -43,13 +42,15 @@
         near = (source - target <= around) & (target - source <= around)
         return near | ((source >= low) & (source < high))
 
-    peers = [lax.rem(me_r + k, rows) for k in range(1, rows)]
+    def related(r):
+        return takes(me_r, r) | takes(r, me_r)
+
     barrier = pltpu.get_barrier_semaphore()
-    for peer in peers:
-
-        @pl.when(takes(peer, me_r))
-        def _(peer=peer):
-            pl.semaphore_signal(barrier, inc=1, device_id={"row": peer}, device_id_type=MESH)
+    for r in range(rows):
+
+        @pl.when((r > me_r) & related(r))
+        def _(r=r):
+            pl.semaphore_signal(barrier, inc=1, device_id={"row": r}, device_id_type=MESH)
 
     pairs = (
         (res_hbm, res_ref.at[me_r]), (table_hbm, table_ref), (w1_hbm, w1_ref), (pw_hbm, pw_ref),
@@ -59,24 +60,36 @@
     for load in loads:
         load.start()
 
-    expected = sum(takes(me_r, peer).astype(jnp.int32) for peer in peers)
-    pl.semaphore_wait(barrier, expected)
+    greeted = sum(((r < me_r) & related(r)).astype(jnp.int32) for r in range(rows))
+
+    @pl.when(me_r > 0)
+    def _():
+        pl.semaphore_wait(barrier, greeted)
+
+    for r in range(rows):
+
+        @pl.when((r < me_r) & takes(r, me_r))
+        def _(r=r):
+            pl.semaphore_signal(
+                ready.at[me_r], inc=1, device_id={"row": r}, device_id_type=MESH
+            )
+
     copies = [
         pltpu.make_async_remote_copy(
             src_ref=res_hbm,
             dst_ref=res_ref.at[me_r],
-            send_sem=send_sem.at[k],
-            recv_sem=recv_sem.at[k],
-            device_id={"row": peer},
+            send_sem=send_sem.at[r],
+            recv_sem=recv_sem.at[me_r],
+            device_id={"row": r},
             device_id_type=MESH,
         )
-        for k, peer in enumerate(peers)
+        for r in range(rows)
     ]
-    for copy, peer in zip(copies, peers):
-
-        @pl.when(takes(me_r, peer))
-        def _(copy=copy):
-            copy.start()
+    for r in range(rows):
+
+        @pl.when((r < me_r) & takes(me_r, r))
+        def _(r=r):
+            copies[r].start()
 
     slot = 1 << (vocab - 1).bit_length()
     share = 128 // slot
@@ -102,20 +115,34 @@
                     here = 0 <= ty <= 2
                     line.append(w[tap * chans : (tap + 1) * chans] if here else zero)
             bw[layer, g * chans : (g + 1) * chans, :] = jnp.concatenate(line, axis=1)
+    save = pltpu.make_async_copy(bw, bw_out, sems.at[len(pairs)])
+    save.start()
+    for r in range(rows):
+
+        @pl.when((r > me_r) & takes(me_r, r))
+        def _(r=r):
+            pl.semaphore_wait(ready.at[r], 1)
+            copies[r].start()
+
     for load in loads[4:]:
         load.wait()
-
     loads[0].wait()
-    for k, copy in enumerate(copies):
-        source = lax.rem(me_r + rows - 1 - k, rows)
-
-        @pl.when(takes(source, me_r))
-        def _(copy=copy):
-            copy.wait_recv()
-
-        @pl.when(takes(me_r, peers[k]))
-        def _(copy=copy):
-            copy.wait_send()
+    for r in range(rows):
+
+        @pl.when((r != me_r) & takes(r, me_r))
+        def _(r=r):
+            pltpu.make_async_remote_copy(
+                src_ref=res_hbm,
+                dst_ref=res_ref.at[r],
+                send_sem=send_sem.at[r],
+                recv_sem=recv_sem.at[r],
+                device_id={"row": r},
+                device_id_type=MESH,
+            ).wait_recv()
+
+        @pl.when((r != me_r) & takes(me_r, r))
+        def _(r=r):
+            copies[r].wait_send()
 
     shards = [me_r + i - around for i in range(n_row // span)]
     shards += [low + i for i in range(n_col // span)]
@@ -190,17 +217,18 @@
     slabs = wide // STRIPS
     for m in range(slabs):
         right_out[STRIPS * m : STRIPS * (m + 1)] = right_ref[pl.ds(m, STRIPS, stride=slabs), :]
+    save.wait()
 
 
 def pair_kernel(
-    dims, left_hbm, right_hbm, bw_hbm, out_hbm, left_ref, right_ref, bw, pair, act_a, act_b, lin, stage, outv, masks, sems
+    dims, left_ref, right_ref, bw_hbm, out_hbm, bw, pair, act_a, act_b, lin, stage, outv, masks, sems
 ):
     rows, ncol, span, tile, chans, layers = dims
     me_r, me_c = lax.axis_index("row"), lax.axis_index("col")
     n_pair = (span + 2 * HALO) // 2
     wide, two = tile + 2 * HALO, 2 * chans
     slabs = wide // STRIPS
-    moves = ((left_hbm, left_ref), (right_hbm, right_ref), (bw_hbm, bw))
+    moves = ((bw_hbm, bw),)
     loads = [pltpu.make_async_copy(a, b, sems.at[i]) for i, (a, b) in enumerate(moves)]
     for load in loads:
         load.start()
@@ -255,8 +283,6 @@
             values.append(pair[p] + total)
         return values
 
-    loads[0].wait()
-    loads[1].wait()
     bufs = (act_a, act_b)
     for layer in range(layers - 1):
         src, dst = bufs[layer % 2], bufs[(layer + 1) % 2]
@@ -267,7 +293,7 @@
                 return 0
 
             lax.fori_loop(0, n_pair, begin, 0, unroll=4)
-            loads[2].wait()
+            loads[0].wait()
 
         def step(q, _, rim=False, layer=layer, src=src, dst=dst, d=d):
             if rim:
@@ -296,6 +322,7 @@
     src = bufs[(layers - 1) % 2]
     d = 2 ** (layers - 1)
     halves = tile // 128
+    saves = []
     for u in range((n_pair - HALO) // 2):
         slots = (HALO // 2 + 2 * u, HALO // 2 + 2 * u + 1)
         for k, value in enumerate(conv(layers - 1, src, d, slots)):
@@ -309,17 +336,16 @@
                 block = turned[:, 128 * h : 128 * (h + 1)]
                 for i, rows_of in ((line, block[0:chans]), (line + d, block[chans:two])):
                     stage[h, i // 16, pl.ds(i % 16, chans, stride=STEP), :] = rows_of
-    step = chans // CHUNKS
-    saves = []
-    for g in range(CHUNKS):
-        for c in range(g * step, (g + 1) * step):
-            for h in range(halves):
-                for r in range(span // 16):
-                    got = stage[h, r, STEP * c : STEP * c + 16, :]
-                    outv[c, 16 * r : 16 * (r + 1), 128 * h : 128 * (h + 1)] = got.astype(BF16)
-        part = pl.ds(g * step, step)
-        saves.append(pltpu.make_async_copy(outv.at[part], out_hbm.at[part], sems.at[3 + g]))
-        saves[-1].start()
+        if (2 * u + 2) % d == 0:
+            group = 2 * d
+            r = (2 * u + 2) // d - 1
+            for c in range(chans):
+                for h in range(halves):
+                    got = stage[h, r, STEP * c : STEP * c + group, :]
+                    outv[c, group * r : group * (r + 1), 128 * h : 128 * (h + 1)] = got.astype(BF16)
+            part = pl.ds(group * r, group)
+            saves.append(pltpu.make_async_copy(outv.at[:, part], out_hbm.at[:, part], sems.at[1 + r]))
+            saves[-1].start()
     for save in saves:
         save.wait()
 
@@ -344,12 +370,12 @@
     left, right, weights = pl.pallas_call(
         functools.partial(sequence_kernel, (rows, ncol, span, tile, chans, kernel, layers)),
         out_shape=(
-            jax.ShapeDtypeStruct((n_pair, two), F32),
-            jax.ShapeDtypeStruct((wide, two), F32),
+            pltpu.VMEM((n_pair, two), F32),
+            pltpu.VMEM((wide, two), F32),
             jax.ShapeDtypeStruct((layers, 4 * chans, 6 * chans), BF16),
         ),
         in_specs=[hbm] * 7,
-        out_specs=(vmem, vmem, vmem),
+        out_specs=(vmem, vmem, hbm),
         scratch_shapes=[
             pltpu.VMEM((rows, 1, span), jnp.int32),
             pltpu.VMEM(embed_table.shape, BF16),
@@ -358,27 +384,29 @@
             pltpu.VMEM((chans, width), BF16),
             pltpu.VMEM((chans, width), BF16),
             pltpu.VMEM(pair_weights.shape, BF16),
-            pltpu.SemaphoreType.DMA((7,)),
+            pltpu.SemaphoreType.DMA((8,)),
             pltpu.SemaphoreType.DMA((rows,)),
             pltpu.SemaphoreType.DMA((rows,)),
+            pltpu.SemaphoreType.REGULAR((rows,)),
             pltpu.VMEM((-(-kernel * slot // 128) * 128, width), BF16),
             pltpu.VMEM((padded, width), F32),
             pltpu.VMEM((padded, two), F32),
             pltpu.VMEM((wide, two), F32),
+            pltpu.VMEM((layers, 4 * chans, 6 * chans), BF16),
         ],
         compiler_params=pltpu.CompilerParams(
             vmem_limit_bytes=LIMIT, collective_id=0, has_side_effects=True
         ),
         name="sequence",
     )(residues.reshape(1, span), embed_table, conv_first, conv_second, proj_row.T, proj_col.T, pair_weights)
+    left = pltpu.with_memory_space_constraint(left, pltpu.VMEM)
+    right = pltpu.with_memory_space_constraint(right, pltpu.VMEM)
     return pl.pallas_call(
         functools.partial(pair_kernel, (rows, ncol, span, tile, chans, layers)),
         out_shape=jax.ShapeDtypeStruct((chans, span, tile), BF16),
-        in_specs=[hbm] * 3,
+        in_specs=[vmem, vmem, hbm],
         out_specs=hbm,
         scratch_shapes=[
-            pltpu.VMEM((n_pair, two), F32),
-            pltpu.VMEM((wide, two), F32),
             pltpu.VMEM((layers, 4 * chans, 6 * chans), BF16),
             pltpu.VMEM((n_pair, wide, two), F32),
             pltpu.VMEM((n_pair, wide, two), BF16),
@@ -387,9 +415,9 @@
             pltpu.VMEM((tile // 128, span // 16, chans * STEP, 128), F32),
             pltpu.VMEM((chans, span, tile), BF16),
             pltpu.VMEM((3, wide, two), BF16),
-            pltpu.SemaphoreType.DMA((3 + CHUNKS,)),
+            pltpu.SemaphoreType.DMA((1 + span // 16,)),
         ],
-        compiler_params=pltpu.CompilerParams(vmem_limit_bytes=LIMIT),
+        compiler_params=pltpu.CompilerParams(vmem_limit_bytes=LIMIT - 409600),
         name="pairs",
     )(left, right, weights)
 

time: 26 us -> 23.5 us (0.904)
  Pallas kernels: 25.8 us -> 23.3 us
    pallas_call x1, Pallas kernels: 12 us -> 10.4 us  [local(): pl.pallas_call(functools.partial(sequence_kernel, (rows, ncol, span, tile...]
    pallas_call x1, Pallas kernels: 13.8 us -> 12.9 us  [local(): pl.pallas_call(functools.partial(pair_kernel, (rows, ncol, span, tile, ch...]
where the time goes in v2:
time: 23.5 us; the launch traced here: 23.3 us
  Pallas kernels  23.3 us (99%)
    pallas_call x1, Pallas kernels, local(): pl.pallas_call(functools.partial(pair_kernel, (rows, ncol, span, tile, ch...  12.9 us
    pallas_call x1, Pallas kernels, local(): pl.pallas_call(functools.partial(sequence_kernel, (rows, ncol, span, tile...  10.4 us

profile of v2, /device:TPU:0, one launch (start us, length us, event | category | flops | bytes accessed | tf_op | source)
XLA Modules:
  0.0 23.3 jit_solution(7447738123269099950)
XLA Ops:
  0.0 10.4 %sequence.1 = (f32[32,128]{1,0:T(8,128)S(1)}, f32[288,128]{1,0:T(8,128)S(1)}, bf16[4,256,384]{2,1,0:T(8,128)(2,1)}) custom-call(s32[1,32]{1,0:T(1,128)} %bitcast.5, bf16[21,256]{1,0:T(8,128)(2,1)} %table_hbm.1, bf16[4352,256]{1,0:T(8,128)(2,1)} %w1_hbm.1, bf16[4352,256]{1,0:T(8,128)(2,1)} %w2_hbm.1, bf16[64,256]{1,0:T(8,128)(2,1)} %bitcast.3, ...), custom_call_target="tpu_custom_call" | custom-call | tf_op jit(solution)/shard_map/sequence/pallas_call | solution.py:370
  10.4 12.9 %pairs.1 = bf16[64,32,256]{2,1,0:T(8,128)(2,1)} custom-call(f32[32,128]{1,0:T(8,128)S(1)} %get-tuple-element.8.left_ref, f32[288,128]{1,0:T(8,128)S(1)} %get-tuple-element.9.right_ref, bf16[4,256,384]{2,1,0:T(8,128)(2,1)} %get-tuple-element.10.bw_hbm), custom_call_target="tpu_custom_call" | custom-call | tf_op jit(solution)/shard_map/pairs/pallas_call | solution.py:404

commit v3 on v2

--- a/solution.py
+++ b/solution.py
@@ -9,6 +9,7 @@
 
 MESH = pl.DeviceIdType.MESH
 STRIPS = 16
+GROUP = 4
 STEP = 18
 LIMIT = 67043328 - 163840
 TAPS = 4
@@ -18,6 +19,14 @@
 
 def elu(v):
     return jnp.maximum(v, jnp.exp(jnp.minimum(v, 0.0)) - 1.0)
+
+
+def turned_over(layer, block, t):
+    return block % 2 if layer % 2 == 0 else int(t >= 2 ** (layer - 1))
+
+
+def swaps(layer, f):
+    return 1 - f if layer % 2 == 0 else f
 
 
 def sequence_kernel(
@@ -106,15 +115,17 @@
     zero = jnp.zeros((chans, chans), BF16)
     for layer in range(layers):
         w = pw_ref[layer].astype(F32).T.astype(BF16)
-        for g, offset in enumerate((0, 1, 2, -1)):
-            line = []
-            for tx in range(3):
-                for h in range(2):
-                    ty = offset - h + 1
-                    tap = 3 * ty + tx
-                    here = 0 <= ty <= 2
-                    line.append(w[tap * chans : (tap + 1) * chans] if here else zero)
-            bw[layer, g * chans : (g + 1) * chans, :] = jnp.concatenate(line, axis=1)
+        for f in range(2):
+            beside = (2, -1) if swaps(layer, f) == 0 else (-1, 2)
+            for g, offset in enumerate(((0, 1) if f == 0 else (1, 0)) + beside):
+                line = []
+                for tx in range(3):
+                    for h in (0, 1) if f == 0 else (1, 0):
+                        ty = offset - h + 1
+                        tap = 3 * ty + tx
+                        here = 0 <= ty <= 2
+                        line.append(w[tap * chans : (tap + 1) * chans] if here else zero)
+                bw[layer, f, g * chans : (g + 1) * chans, :] = jnp.concatenate(line, axis=1)
     save = pltpu.make_async_copy(bw, bw_out, sems.at[len(pairs)])
     save.start()
     for r in range(rows):
@@ -211,6 +222,8 @@
     right_ref[...] = project(second[height : height + wide], pcol_ref[...])
     n_pair = height // 2
     half_lane = lax.broadcasted_iota(jnp.int32, (n_pair, two), 1) < chans
+    odd = lax.rem(lax.broadcasted_iota(jnp.int32, (n_pair, two), 0), 2) == 1
+    half_lane = half_lane != odd
     left_out[...] = jnp.where(
         half_lane, tmp[pl.ds(0, n_pair, stride=2), :], tmp[pl.ds(1, n_pair, stride=2), :]
     )
@@ -241,46 +254,69 @@
     masks[1] = (inside * (me_r > 0).astype(F32)).astype(BF16)
     masks[2] = (inside * (me_r < rows - 1).astype(F32)).astype(BF16)
     lane = lax.broadcasted_iota(jnp.int32, (wide, two), 1)
+    lane = lane[0:STRIPS]
     low_bf16 = lane.astype(F32).astype(BF16) < jnp.asarray(chans, BF16)
     low_half = lane < chans
 
     def put(act, p, value):
         pair[p] = value
-        if isinstance(p, int):
-            which = 1 if p < HALO // 2 else 2 if p >= n_pair - HALO // 2 else 0
-        else:
-            which = jnp.where(p < HALO // 2, 1, jnp.where(p >= n_pair - HALO // 2, 2, 0))
+        which = jnp.where(p < HALO // 2, 1, jnp.where(p >= n_pair - HALO // 2, 2, 0))
         act[p] = elu(value).astype(BF16) * masks[which]
 
     def start(p):
         put(act_a, p, right_ref[...] + left_ref[pl.ds(p, 1), :])
 
-    def shifted(part, d):
-        if d > 0:
-            ends = [part[STRIPS * m : STRIPS * (m + 1)] for m in range(slabs - d, slabs)]
-            ends = [pltpu.roll(e, 1, 0) for e in ends]
-            return jnp.concatenate(ends + [part[: STRIPS * (slabs - d)]], axis=0)
-        ends = [part[STRIPS * m : STRIPS * (m + 1)] for m in range(-d)]
-        ends = [pltpu.roll(e, STRIPS - 1, 0) for e in ends]
-        return jnp.concatenate([part[STRIPS * -d :]] + ends, axis=0)
-
-    def conv(layer, src, d, slots):
+    def slab(m):
+        return pl.ds(STRIPS * m, STRIPS)
+
+    def put_slab(act, p, m, value):
+        pair[p, slab(m), :] = value
+        which = 1 if p < HALO // 2 else 2 if p >= n_pair - HALO // 2 else 0
+        act[p, slab(m), :] = elu(value).astype(BF16) * masks[which, slab(m), :]
+
+    def chain(d):
+        return [m for t in range(min(d, slabs)) for m in range(t, slabs, d)]
+
+    def conv(layer, src, d, slots, f):
+        order = chain(d)
+        place = {m: i for i, m in enumerate(order)}
+        after, before = (d, -d) if swaps(layer, f) == 0 else (-d, d)
         lhs = jnp.concatenate(
             [
                 jnp.concatenate(
-                    [src[p], jnp.where(low_bf16, src[p + d], src[p - d])], axis=1
+                    [
+                        src[p, slab(m), :],
+                        jnp.where(low_bf16, src[p + after, slab(m), :], src[p + before, slab(m), :]),
+                    ],
+                    axis=1,
                 )
                 for p in slots
+                for m in order
             ],
             axis=0,
         )
-        got = jnp.dot(lhs, bw[layer], preferred_element_type=F32)
-        values = []
-        for k, p in enumerate(slots):
-            part = got[k * wide : (k + 1) * wide]
-            total = shifted(part[:, 0:two], d) + part[:, two : 2 * two]
-            total = total + shifted(part[:, 2 * two : 3 * two], -d)
-            values.append(pair[p] + total)
+        got = jnp.dot(lhs, bw[layer, f], preferred_element_type=F32)
+
+        def piece(k, m, tx):
+            at = k * wide + STRIPS * place[m % slabs]
+            part = got[at : at + STRIPS, tx * two : (tx + 1) * two]
+            if m < 0:
+                return pltpu.roll(part, 1, 0)
+            return part if m < slabs else pltpu.roll(part, STRIPS - 1, 0)
+
+        def value(p, m):
+            k = slots.index(p)
+            total = piece(k, m - d, 0) + piece(k, m, 1) + piece(k, m + d, 2)
+            return pair[p, slab(m), :] + total
+
+        return {p: value for p in slots}
+
+    def convs(layer, src, d, slots):
+        values = {}
+        for f in range(2):
+            some = [p for p in slots if turned_over(layer, p // d, p % d) == f]
+            if some:
+                values.update(conv(layer, src, d, some, f))
         return values
 
     bufs = (act_a, act_b)
@@ -295,46 +331,63 @@
             lax.fori_loop(0, n_pair, begin, 0, unroll=4)
             loads[0].wait()
 
-        def step(q, _, rim=False, layer=layer, src=src, dst=dst, d=d):
-            if rim:
-                slots = [q + d, n_pair - 2 * d + q]
-            else:
-                x = 2 * d * lax.div(q, d) + lax.rem(q, d)
-                slots = [x, x + d]
-            one, other = conv(layer, src, d, slots)
-            if rim:
-                new = [pltpu.roll(one, chans, 1), one, other, pltpu.roll(other, chans, 1)]
-                slots = [q, q + d, n_pair - 2 * d + q, n_pair - d + q]
-            else:
-                new = [
-                    jnp.where(low_half, one, pltpu.roll(other, chans, 1)),
-                    jnp.where(low_half, pltpu.roll(one, chans, 1), other),
-                ]
-            for p, value in zip(slots, new):
-                put(dst, p, value)
-            return 0
-
-        n_main = n_pair // 2 - 2 * d
-        lax.fori_loop(d, d + n_main, step, 0, unroll=n_main // 2)
-        for q in range(d):
-            step(q, 0, rim=True)
+        def place(layer, d, r, x):
+            low_here = (r % 2) == turned_over(layer, x // d + r // 2, x % d)
+            target = x + (r % 2) * d
+            over = turned_over(layer + 1, target // (2 * d), target % (2 * d))
+            return target, (r // 2) == over, low_here
+
+        units = [(q + d,) for q in range(d)] + [(n_pair - 2 * d + q,) for q in range(d)]
+        for q in range(d, n_pair // 2 - d):
+            x = 2 * d * (q // d) + q % d
+            units.append((x, x + d))
+        for i, unit in enumerate(units):
+            if i % GROUP == 0:
+                some = units[i : i + GROUP]
+                values = convs(layer, src, d, [p for each in some for p in each])
+            x = 2 * d * (unit[0] // (2 * d)) + unit[0] % d
+            rows_in = [2 * ((p - x) // d) + j for p in unit for j in range(2)]
+            for m in chain(d):
+                got = {p: values[p](p, m) for p in unit}
+                moved = {}
+                new = {}
+                for r in rows_in:
+                    p = x + (r // 2) * d
+                    target, low_there, low_here = place(layer, d, r, x)
+                    if low_there == low_here:
+                        v = got[p]
+                    else:
+                        if p not in moved:
+                            moved[p] = pltpu.roll(got[p], chans, 1)
+                        v = moved[p]
+                    new.setdefault(target, {})[low_there] = v
+                for target, sides in new.items():
+                    if len(sides) == 2:
+                        v = jnp.where(low_half, sides[True], sides[False])
+                    else:
+                        v = next(iter(sides.values()))
+                    put_slab(dst, target, m, v)
 
     src = bufs[(layers - 1) % 2]
     d = 2 ** (layers - 1)
     halves = tile // 128
     saves = []
+    everyone = list(range(HALO // 2, n_pair - HALO // 2))
+    values = convs(layers - 1, src, d, everyone)
     for u in range((n_pair - HALO) // 2):
         slots = (HALO // 2 + 2 * u, HALO // 2 + 2 * u + 1)
-        for k, value in enumerate(conv(layers - 1, src, d, slots)):
+        for k, p in enumerate(slots):
             b = lin.at[(2 * u + k) % 4]
-            for m in range(slabs):
-                b[pl.ds(m, STRIPS, stride=slabs), :] = value[STRIPS * m : STRIPS * (m + 1)]
+            for m in chain(d):
+                b[pl.ds(m, STRIPS, stride=slabs), :] = values[p](p, m)
             turned = b[HALO : HALO + tile, :].T
-            at = slots[k] - HALO // 2
+            at = p - HALO // 2
             line = 2 * d * (at // d) + at % d
             for h in range(halves):
                 block = turned[:, 128 * h : 128 * (h + 1)]
-                for i, rows_of in ((line, block[0:chans]), (line + d, block[chans:two])):
+                over = turned_over(layers - 1, p // d, p % d)
+                ends = (line + d, line) if over else (line, line + d)
+                for i, rows_of in ((ends[0], block[0:chans]), (ends[1], block[chans:two])):
                     stage[h, i // 16, pl.ds(i % 16, chans, stride=STEP), :] = rows_of
         if (2 * u + 2) % d == 0:
             group = 2 * d
@@ -372,7 +425,7 @@
         out_shape=(
             pltpu.VMEM((n_pair, two), F32),
             pltpu.VMEM((wide, two), F32),
-            jax.ShapeDtypeStruct((layers, 4 * chans, 6 * chans), BF16),
+            jax.ShapeDtypeStruct((layers, 2, 4 * chans, 6 * chans), BF16),
         ),
         in_specs=[hbm] * 7,
         out_specs=(vmem, vmem, hbm),
@@ -392,7 +445,7 @@
             pltpu.VMEM((padded, width), F32),
             pltpu.VMEM((padded, two), F32),
             pltpu.VMEM((wide, two), F32),
-            pltpu.VMEM((layers, 4 * chans, 6 * chans), BF16),
+            pltpu.VMEM((layers, 2, 4 * chans, 6 * chans), BF16),
         ],
         compiler_params=pltpu.CompilerParams(
             vmem_limit_bytes=LIMIT, collective_id=0, has_side_effects=True
@@ -407,7 +460,7 @@
         in_specs=[vmem, vmem, hbm],
         out_specs=hbm,
         scratch_shapes=[
-            pltpu.VMEM((layers, 4 * chans, 6 * chans), BF16),
+            pltpu.VMEM((layers, 2, 4 * chans, 6 * chans), BF16),
             pltpu.VMEM((n_pair, wide, two), F32),
             pltpu.VMEM((n_pair, wide, two), BF16),
             pltpu.VMEM((n_pair, wide, two), BF16),

time: 23.5 us -> 22.6 us (0.962)
  Pallas kernels: 23.3 us -> 22.4 us
    pallas_call x1, Pallas kernels: 12.9 us -> 12 us  [local(): pl.pallas_call(functools.partial(pair_kernel, (rows, ncol, span, tile, ch...]
where the time goes in v3:
time: 22.6 us; the launch traced here: 22.4 us
  Pallas kernels  22.4 us (99%)
    pallas_call x1, Pallas kernels, local(): pl.pallas_call(functools.partial(pair_kernel, (rows, ncol, span, tile, ch...  12 us
    pallas_call x1, Pallas kernels, local(): pl.pallas_call(functools.partial(sequence_kernel, (rows, ncol, span, tile...  10.4 us

profile of v3, /device:TPU:0, one launch (start us, length us, event | category | flops | bytes accessed | tf_op | source)
XLA Modules:
  0.0 22.4 jit_solution(1412576983188956612)
XLA Ops:
  0.0 10.4 %sequence.1 = (f32[32,128]{1,0:T(8,128)S(1)}, f32[288,128]{1,0:T(8,128)S(1)}, bf16[4,2,256,384]{3,2,1,0:T(8,128)(2,1)}) custom-call(s32[1,32]{1,0:T(1,128)} %bitcast.5, bf16[21,256]{1,0:T(8,128)(2,1)} %table_hbm.1, bf16[4352,256]{1,0:T(8,128)(2,1)} %w1_hbm.1, bf16[4352,256]{1,0:T(8,128)(2,1)} %w2_hbm.1, bf16[64,256]{1,0:T(8,128)(2,1)} %bitcast.3, ...), custom_call_target="tpu_custom_call" | custom-call | tf_op jit(solution)/shard_map/sequence/pallas_call | solution.py:423
  10.4 12.0 %pairs.1 = bf16[64,32,256]{2,1,0:T(8,128)(2,1)} custom-call(f32[32,128]{1,0:T(8,128)S(1)} %get-tuple-element.8.left_ref, f32[288,128]{1,0:T(8,128)S(1)} %get-tuple-element.9.right_ref, bf16[4,2,256,384]{3,2,1,0:T(8,128)(2,1)} %get-tuple-element.10.bw_hbm), custom_call_target="tpu_custom_call" | custom-call | tf_op jit(solution)/shard_map/pairs/pallas_call | solution.py:457
